TPU v7x, 256 devices: a whole 4x4x8 slice. The times are simulated.
256 devices in a mesh: subj: 8 (over y_hi, x), cortex: 32 (over y_lo, z, core).
Axes of the slice: x: 4, y: 4 (y_hi: 2, y_lo: 2; y = y_hi * 2 + y_lo), z: 8, core: 2. Of those that a mesh axis runs over, the one named last changes fastest.
Arguments:
- series: bfloat16 [16, 1024, 8192], P('subj', None, 'cortex'), may hold values from -6 to 6
- template: bfloat16 [1024, 8192], P(None, 'cortex'), may hold values from -6 to 6
- sl_blocks: int32 [64, 3], P('cortex'), may hold values from 0 to 63, as said below
Outputs:
- template_new: float32 [1024, 8192], P(None, 'cortex')
Inputs may be any that keep to these rules, and one draw needn't show every extreme that they name: sl_blocks[g, 0] = g; the other two entries of row g are distinct, differ from g, and lie between (g // 2 - 1) * 2 and (g // 2 + 2) * 2 - 1.
All inputs are finite; a program needn't handle non-finite values.
Results may differ from a plain program's by a relative error of at most 0.0024.
Values may be sent and summed in bfloat16 or wider, within the bound.
A program may use at most 64 MiB of HBM per device.

v0:
```python
import jax
import jax.numpy as jnp
from jax import lax
from jax.sharding import PartitionSpec as P

BLOCK = 128
NS_STEPS = 8
BLK_DEV = 2


RIDGE_SHIFT = 0.1
NORM_EPSILON = 1e-06


def with_halo(cells, sides, width):
    for axis, dim in sides:
        count = lax.axis_size(axis)
        ends = count - 1
        head = lax.slice_in_dim(cells, 0, width, axis=dim)
        tail = lax.slice_in_dim(cells, cells.shape[dim] - width, cells.shape[dim], axis=dim)
        cells = jnp.concatenate(
            [
                lax.ppermute(tail, axis, [(i, (i + 1) % count) for i in range(ends)]),
                cells,
                lax.ppermute(head, axis, [((i + 1) % count, i) for i in range(ends)]),
            ],
            axis=dim,
        )
    return cells


def in_order(tiles, dim):
    shape = list(tiles.shape[1:])
    shape[dim] *= tiles.shape[0]
    return jnp.moveaxis(tiles, 0, dim).reshape(shape)


def copy_for_each(x, axis):
    length = lax.axis_size(axis)
    return lax.all_to_all(jnp.broadcast_to(x[None], (length, *x.shape)), axis, 0, 0, tiled=True)


def gathered_copies(x, axis, dim):
    return in_order(copy_for_each(x, axis), dim)


def from_behind(block, axis, distance):
    devices = range(lax.axis_size(axis))
    route = [(i - distance, i) for i in devices if i - distance in devices]
    return lax.ppermute(block, axis, route)


def body(series, template, sl_blocks):
    subj_count = series.shape[0]
    frame_count = series.shape[1]
    width_dev = series.shape[2]
    halo_data = with_halo(series, (("cortex", 2),), width_dev)
    halo_tmpl = with_halo(template, (("cortex", 1),), width_dev)
    all_lists = gathered_copies(sl_blocks, "cortex", 0)
    position = lax.axis_index("cortex")
    window_blocks = 3 * BLK_DEV
    window_ids = (sl_blocks - (position - 1) * BLK_DEV).reshape(-1)
    data_blocks = halo_data.reshape(subj_count, frame_count, window_blocks, BLOCK)
    tmpl_blocks = halo_tmpl.reshape(frame_count, window_blocks, BLOCK)
    subj_tiles = jnp.take(data_blocks, window_ids, axis=2).reshape(
        subj_count, frame_count, BLK_DEV, 3 * BLOCK
    )
    tmpl_tiles = jnp.take(tmpl_blocks, window_ids, axis=1).reshape(frame_count, BLK_DEV, 3 * BLOCK)
    identity = jnp.eye(3 * BLOCK, dtype=jnp.float32)
    cross_prod = jnp.einsum(
        "sfka,fkb->skab", subj_tiles, tmpl_tiles, preferred_element_type=jnp.float32
    )
    cross_prod = cross_prod / frame_count + RIDGE_SHIFT * identity
    squares = jnp.sum(cross_prod * cross_prod, axis=(2, 3), keepdims=True)
    polar_map = (cross_prod / jnp.sqrt(squares + NORM_EPSILON)).astype(jnp.bfloat16)
    for iteration in range(NS_STEPS):
        gram_mat = jnp.einsum(
            "skab,skac->skbc", polar_map, polar_map, preferred_element_type=jnp.float32
        ).astype(jnp.bfloat16)
        product = jnp.einsum(
            "skab,skbc->skac", polar_map, gram_mat, preferred_element_type=jnp.float32
        )
        polar_map = (1.5 * polar_map.astype(jnp.float32) - 0.5 * product).astype(jnp.bfloat16)
    mapped = jnp.einsum(
        "sfka,skab->sfkb", subj_tiles, polar_map, preferred_element_type=jnp.float32
    )
    tiles = mapped.reshape(subj_count, frame_count, BLK_DEV * 3, BLOCK)
    one_hot = (window_ids[:, None] == jnp.arange(window_blocks, dtype=jnp.int32)[None, :]).astype(
        jnp.float32
    )
    window_sum = jnp.einsum("sfjc,jw->sfwc", tiles, one_hot, precision=lax.Precision.HIGHEST)
    window_sum = window_sum.reshape(subj_count, frame_count, 3, width_dev)
    mine = position * BLK_DEV + jnp.arange(BLK_DEV, dtype=jnp.int32)
    block_ids = all_lists.reshape(-1)
    coverage = jnp.sum((block_ids[:, None] == mine[None, :]).astype(jnp.float32), axis=0)
    per_vertex = jnp.repeat(coverage, BLOCK)
    subject_sum = jnp.sum(window_sum, axis=0)
    from_lower = from_behind(subject_sum[:, 2].astype(jnp.bfloat16), "cortex", 1).astype(
        jnp.float32
    )
    from_upper = from_behind(subject_sum[:, 0].astype(jnp.bfloat16), "cortex", -1).astype(
        jnp.float32
    )
    own_sum = subject_sum[:, 1] + from_lower + from_upper
    averaged = own_sum / per_vertex[None, :]
    combined = lax.psum(averaged, "subj")
    return combined / (subj_count * lax.axis_size("subj"))


def solution(mesh):
    in_specs = (P("subj", None, "cortex"), P(None, "cortex"), P("cortex", None))
    out_specs = P(None, "cortex")
    return jax.shard_map(body, mesh=mesh, in_specs=in_specs, out_specs=out_specs, check_vma=False)
```

profile of v0, /device:TPU:2, one launch (start us, length us, event | category | flops | bytes accessed | tf_op | source)
XLA Modules:
  0.0 221.9 jit_solution(2787901281315363890)
XLA Ops:
  6.5 1.3 copy.147
  7.9 1.3 collective-permute-start.1
  9.2 3.8 %collective-permute-start = (bf16[1024,256]{0,1:T(8,128)(2,1)S(1)}, bf16[1024,256]{0,1:T(8,128)(2,1)}, u32[]{:S(2)}, u32[]{:S(2)}) collective-permute-start(bf16[1024,256]{0,1:T(8,128)(2,1)S(1)} %copy.147), channel_id=1, source_target_pairs={{0,1},{1,2},{2,3},{3,4},{4,5},{5,6},{6,7},{7,8},{8,9},{9,10},{10,1... | collective-permute-start | bytes 1572872 | tf_op jit(solution)/shard_map/ppermute | solution.py:23
  13.0 1.3 copy.152
  14.3 1.3 collective-permute-start.3
  15.6 4.3 %collective-permute-start.2 = (bf16[2,1024,256]{1,2,0:T(8,128)(2,1)}, bf16[2,1024,256]{1,2,0:T(8,128)(2,1)}, u32[]{:S(2)}, u32[]{:S(2)}) collective-permute-start(bf16[2,1024,256]{1,2,0:T(8,128)(2,1)} %copy.152), channel_id=1, source_target_pairs={{0,1},{1,2},{2,3},{3,4},{4,5},{5,6},{6,7},{7,8},{8,9},{9,10},{10,1... | collective-permute-start | bytes 3145736 | tf_op jit(solution)/shard_map/ppermute | solution.py:23
  19.9 0.1 broadcast_bitcast_fusion
  20.0 0.1 reshape.83
  20.1 0.1 eq.37
  20.2 0.9 fusion.24
  21.1 0.0 collective-permute-done.1
  21.1 0.8 copy-done.3
  21.8 0.0 collective-permute-done
  21.8 1.3 pad_maximum_fusion.1
  23.2 0.9 copy.150
  24.1 0.8 gather_fusion
  24.9 0.7 copy.151
  25.6 1.4 bitcast_select_fusion.1
  27.0 0.0 collective-permute-done.3
  27.0 3.1 %pad_maximum_fusion = bf16[2,1024,768]{1,2,0:T(8,128)(2,1)} fusion(bf16[2,1024,256]{1,2,0:T(8,128)(2,1)} %collective-permute-done.3, bf16[2,1024,256]{1,2,0:T(8,128)(2,1)} %copy.152, bf16[2,1024,256]{1,2,0:T(8,128)(2,1)} %collective-permute-done.2), kind=kLoop, calls=%fused_computation.2 | loop fusion | flops 9437184 | bytes 6291456 | tf_op jit(solution)/shard_map/concatenate | solution.py:21
  30.1 3.5 %copy.155 = bf16[2,1024,6,128]{3,1,2,0:T(8,128)(2,1)S(1)} copy(bf16[2,1024,6,128]{1,3,2,0:T(8,128)(2,1)} %bitcast.71) | data formatting | bytes 6291456 | tf_op jit(solution)/shard_map/reshape | solution.py:63
  33.6 2.7 %gather_fusion.1 = bf16[6,2,1024,128]{3,2,1,0:T(8,128)(2,1)} fusion(bf16[2,1024,6,128]{3,1,2,0:T(8,128)(2,1)S(1)} %copy.155, s32[1024]{0:T(1024)S(1)} %pad_clamp_fusion), kind=kCustom, calls=%fused_computation.1 | custom fusion | bytes 6291480 | tf_op jit(solution)/shard_map/jit(_take)/gather | solution.py:65
  36.3 3.4 %copy.156 = bf16[2,1024,6,128]{1,3,2,0:T(8,128)(2,1)S(1)} copy(bf16[2,1024,6,128]{3,1,0,2:T(8,128)(2,1)} %bitcast.69) | data formatting | bytes 6291456 | tf_op jit(solution)/shard_map/jit(_take)/gather | solution.py:65
  39.7 0.3 bitcast_select_fusion
  40.1 0.7 copy-done
  40.8 0.5 copy-done.1
  41.3 1.7 multiply_reduce_fusion
  43.0 0.5 divide_convert_fusion
  43.5 0.9 convolution_convert_fusion.7
  44.5 1.0 subtract_convert_fusion.7
  45.5 0.9 convolution_convert_fusion.6
  46.4 1.0 subtract_convert_fusion.6
  47.4 0.9 convolution_convert_fusion.5
  48.3 1.0 subtract_convert_fusion.5
  49.3 0.9 convolution_convert_fusion.4
  50.2 1.0 subtract_convert_fusion.4
  51.2 0.9 convolution_convert_fusion.3
  52.1 1.0 subtract_convert_fusion.3
  53.1 0.9 convolution_convert_fusion.2
  54.1 1.2 subtract_convert_fusion.2
  55.3 0.9 convolution_convert_fusion.1
  56.2 1.0 subtract_convert_fusion.1
  57.2 0.9 convolution_convert_fusion
  58.1 1.0 subtract_convert_fusion
  59.1 4.5 %fusion.10 = f32[2,2,384,1024]{3,2,1,0:T(8,128)} fusion(bf16[2,1024,2,384]{1,3,2,0:T(8,128)(2,1)S(1)} %bitcast_select_fusion, bf16[2,2,384,384]{2,3,0,1:T(8,128)(2,1)S(1)} %subtract_convert_fusion), kind=kOutput, calls=%fused_computation.36 | convolution fusion | flops 1207959552 | bytes 10616832 | tf_op jit(solution)/shard_map/sfka,skab->sfkb/dot_general | solution.py:84
  63.6 8.2 %copy.193 = f32[2,1024,6,128]{3,2,1,0:T(8,128)} copy(f32[2,1024,6,128]{1,3,2,0:T(8,128)} %bitcast.66) | data formatting | bytes 12582912 | tf_op jit(solution)/shard_map/reshape | solution.py:87
  71.9 10.5 %convolution_reduce_fusion = f32[6,1024,128]{2,0,1:T(8,128)} fusion(f32[2,1024,6,128]{3,2,1,0:T(8,128)} %copy.193, s32[6]{0:T(128)S(1)} %eq.37), kind=kOutput, calls=%fused_computation.6 | convolution fusion | flops 114032672 | bytes 9437208 | tf_op jit(solution)/shard_map/sfjc,jw->sfwc/dot_general | solution.py:91
  82.3 3.7 %copy.194 = f32[1024,6,128]{0,2,1:T(8,128)S(1)} copy(f32[1024,6,128]{2,1,0:T(8,128)} %bitcast.70) | data formatting | bytes 6291456 | tf_op jit(solution)/shard_map/reduce_sum | solution.py:97
  86.0 0.2 bitcast_convert_fusion
  86.2 1.0 slice_bitcast_fusion.2
  87.3 8.4 %collective-permute-start.4 = (bf16[1024,256]{0,1:T(8,128)(2,1)}, bf16[1024,256]{0,1:T(8,128)(2,1)}, u32[]{:S(2)}, u32[]{:S(2)}) collective-permute-start(bf16[1024,256]{0,1:T(8,128)(2,1)} %get-tuple-element.7), channel_id=1, source_target_pairs={{0,1},{1,2},{2,3},{3,4},{4,5},{5,6},{6,7},{7,8},{8,9},{9,10},{10,1... | collective-permute-start | bytes 1572872 | tf_op jit(solution)/shard_map/ppermute | solution.py:50
  95.6 1.3 collective-permute-start.5
  96.9 0.6 broadcast_in_dim.43
  97.5 16.7 %all-to-all-start = ((s32[32,2,3]{2,1,0:T(2,128)}), s32[32,2,3]{2,1,0:T(2,128)S(1)}, u32[]{:S(2)}, u32[]{:S(2)}) async-start(s32[32,2,3]{2,1,0:T(2,128)} %broadcast_in_dim.43), calls=%async_computation | async-start | bytes 65536 | tf_op jit(solution)/shard_map/all_to_all | solution.py:40
  114.3 0.0 all-reduce.2.cloned.1.call-start
  114.4 8.5 %all-to-all-done = s32[32,2,3]{2,1,0:T(2,128)S(1)} async-done(((s32[32,2,3]{2,1,0:T(2,128)}), s32[32,2,3]{2,1,0:T(2,128)S(1)}, u32[]{:S(2)}, u32[]{:S(2)}) %all-to-all-start) | async-done | bytes 800 | tf_op jit(solution)/shard_map/all_to_all | solution.py:40
  122.9 0.1 eq.42
  123.0 0.2 fusion.27
  123.2 0.1 broadcast_bitcast_fusion.1
  123.3 2.4 %fusion.23 = f32[1024,256]{0,1:T(8,128)} fusion(f32[1024,3,256]{0,2,1:T(8,128)S(1)} %bitcast.68, bf16[1024,256]{0,1:T(8,128)(2,1)} %collective-permute-done.5, bf16[1024,256]{0,1:T(8,128)(2,1)} %collective-permute-done.4, f32[256]{0:T(256)S(1)} %broadcast_bitcast_fusion.1), kind=kLoop, calls=%fused_computation.50 | loop fusion | flops 1310720 | bytes 3146752 | tf_op jit(solution)/shard_map/div | solution.py:105
  125.7 0.0 all-reduce.2.cloned.1.call-update
  125.7 86.7 %all-reduce.2.cloned.1.call-done = f32[1024,256]{0,1:T(8,128)} async-done(((f32[1024,256]{0,1:T(8,128)}), f32[1024,256]{0,1:T(8,128)}) %all-reduce.2.cloned.1.call-update) | async-done | bytes 1048592 | tf_op jit(solution)/shard_map/psum | solution.py:106
  212.4 1.3 broadcast_multiply_fusion
  213.8 1.3 copy.195
  (16 shorter events, 0.1 us)
Async XLA Ops:
  6.5 6.5 %copy-start.2 = (bf16[2,1024,256]{2,1,0:T(8,128)(2,1)S(1)}, bf16[2,1024,256]{2,1,0:T(8,128)(2,1)}, u32[]{:S(2)}) copy-start(bf16[2,1024,256]{2,1,0:T(8,128)(2,1)} %param.3) | copy-start | bytes 3145732
  6.5 13.4 %copy-start.4 = (s32[2,3]{1,0:T(2,128)S(1)}, s32[2,3]{1,0:T(2,128)}, u32[]{:S(2)}) copy-start(s32[2,3]{1,0:T(2,128)} %param.5) | copy-start | bytes 76
  7.9 13.2 %collective-permute-start.1 = (bf16[1024,256]{0,1:T(8,128)(2,1)S(1)}, bf16[1024,256]{0,1:T(8,128)(2,1)S(1)}, u32[]{:S(2)}, u32[]{:S(2)}) collective-permute-start(bf16[1024,256]{0,1:T(8,128)(2,1)S(1)} %copy.147), channel_id=1, source_target_pairs={{1,0},{2,1},{3,2},{4,3},{5,4},{6,5},{7,6},{8,7},{9,8},{10,9},{11,1... | collective-permute-start | bytes 1572872 | tf_op jit(solution)/shard_map/ppermute | solution.py:25
  9.2 12.7 %collective-permute-start = (bf16[1024,256]{0,1:T(8,128)(2,1)S(1)}, bf16[1024,256]{0,1:T(8,128)(2,1)}, u32[]{:S(2)}, u32[]{:S(2)}) collective-permute-start(bf16[1024,256]{0,1:T(8,128)(2,1)S(1)} %copy.147), channel_id=1, source_target_pairs={{0,1},{1,2},{2,3},{3,4},{4,5},{5,6},{6,7},{7,8},{8,9},{9,10},{10,1... | collective-permute-start | bytes 1572872 | tf_op jit(solution)/shard_map/ppermute | solution.py:23
  14.3 12.7 %collective-permute-start.3 = (bf16[2,1024,256]{1,2,0:T(8,128)(2,1)}, bf16[2,1024,256]{1,2,0:T(8,128)(2,1)}, u32[]{:S(2)}, u32[]{:S(2)}) collective-permute-start(bf16[2,1024,256]{1,2,0:T(8,128)(2,1)} %copy.152), channel_id=1, source_target_pairs={{1,0},{2,1},{3,2},{4,3},{5,4},{6,5},{7,6},{8,7},{9,8},{10,9},{11,1... | collective-permute-start | bytes 3145736 | tf_op jit(solution)/shard_map/ppermute | solution.py:25
  15.6 11.4 %collective-permute-start.2 = (bf16[2,1024,256]{1,2,0:T(8,128)(2,1)}, bf16[2,1024,256]{1,2,0:T(8,128)(2,1)}, u32[]{:S(2)}, u32[]{:S(2)}) collective-permute-start(bf16[2,1024,256]{1,2,0:T(8,128)(2,1)} %copy.152), channel_id=1, source_target_pairs={{0,1},{1,2},{2,3},{3,4},{4,5},{5,6},{6,7},{7,8},{8,9},{9,10},{10,1... | collective-permute-start | bytes 3145736 | tf_op jit(solution)/shard_map/ppermute | solution.py:23
  21.1 0.8 copy-start.3
  39.7 1.1 copy-start
  39.7 1.6 copy-start.1
  87.3 36.0 %collective-permute-start.4 = (bf16[1024,256]{0,1:T(8,128)(2,1)}, bf16[1024,256]{0,1:T(8,128)(2,1)}, u32[]{:S(2)}, u32[]{:S(2)}) collective-permute-start(bf16[1024,256]{0,1:T(8,128)(2,1)} %get-tuple-element.7), channel_id=1, source_target_pairs={{0,1},{1,2},{2,3},{3,4},{4,5},{5,6},{6,7},{7,8},{8,9},{9,10},{10,1... | collective-permute-start | bytes 1572872 | tf_op jit(solution)/shard_map/ppermute | solution.py:50
  95.6 27.6 %collective-permute-start.5 = (bf16[1024,256]{0,1:T(8,128)(2,1)}, bf16[1024,256]{0,1:T(8,128)(2,1)}, u32[]{:S(2)}, u32[]{:S(2)}) collective-permute-start(bf16[1024,256]{0,1:T(8,128)(2,1)} %get-tuple-element.8), channel_id=1, source_target_pairs={{1,0},{2,1},{3,2},{4,3},{5,4},{6,5},{7,6},{8,7},{9,8},{10,9},{11,1... | collective-permute-start | bytes 1572872 | tf_op jit(solution)/shard_map/ppermute | solution.py:50
  97.5 25.3 %all-to-all-start = ((s32[32,2,3]{2,1,0:T(2,128)}), s32[32,2,3]{2,1,0:T(2,128)S(1)}, u32[]{:S(2)}, u32[]{:S(2)}) async-start(s32[32,2,3]{2,1,0:T(2,128)} %broadcast_in_dim.43), calls=%async_computation | async-start | bytes 65536 | tf_op jit(solution)/shard_map/all_to_all | solution.py:40
  114.3 98.2 %all-reduce.2.cloned.1.call-start = ((), (), s32[]{:S(2)}) async-start(), calls=%async_computation.1 | async-start | bytes 2097152 | tf_op jit(solution)/shard_map/psum | solution.py:106
Sparse Core Ops, SparseCore 0:
  125.8 86.5 all-reduce.1
where the time goes:
time: 226 us; the launch traced here: 222 us
  waiting for transfers between devices  95.3 us (42%)
  starting transfers between devices  37.2 us (16%)
  matrix products  32.1 us (14%)
  local copies, waits for them, and re-layouts  32 us (14%)
  between operations  13.7 us (6%)
  other arithmetic  11.7 us (5%)
    psum x1, waiting for transfers between devices, body(): combined = lax.psum(averaged, 'subj')  86.7 us
    all_to_all x1, starting transfers between devices, copy_for_each(): lax.all_to_all(jnp.broadcast_to(x[None], (length, *x.shape)), axis, 0, 0,...  16.7 us
    dot_general x1, matrix products, body(): jnp.einsum('sfjc,jw->sfwc', tiles, one_hot, precision=lax.Precision.HIGHEST)  10.5 us
    ppermute x2, starting transfers between devices, from_behind(): return lax.ppermute(block, axis, route)  9.66 us
    all_to_all x1, waiting for transfers between devices, copy_for_each(): lax.all_to_all(jnp.broadcast_to(x[None], (length, *x.shape)), axis, 0, 0,...  8.52 us
    reshape x1, local copies, waits for them, and re-layouts, body(): tiles = mapped.reshape(subj_count, frame_count, BLK_DEV * 3, BLOCK)  8.2 us
    ppermute x2, starting transfers between devices, with_halo(): lax.ppermute(tail, axis, [(i, (i + 1) % count) for i in range(ends)])  8.15 us
    dot_general x8, matrix products, body(): jnp.einsum('skab,skbc->skac', polar_map, gram_mat, preferred_element_type...  8.04 us
  transfers between devices with their start and end apart: 8, of which 2 were waited for; matrix products, arithmetic and copies ran while one was open for 4% of the time, Pallas kernels for 0%

commit v1 on v0

v1 whole, which is shorter than its diff:
```python
import functools

import jax
import jax.numpy as jnp
from jax import lax
from jax.experimental import pallas as pl
from jax.experimental.pallas import tpu as pltpu
from jax.sharding import PartitionSpec as P

BLOCK = 128
NS_STEPS = 8
BLK_DEV = 2
SPAN = 3
WIN = 3 * BLK_DEV
RIDGE_SHIFT = 0.1
NORM_EPSILON = 1e-06
CHUNKS = 4
MESH = pl.DeviceIdType.MESH
LINK = jnp.bfloat16


def kernel(
    subj_devs, cortex_devs, lists, series, template, gathered,
    win_x0, win_x1, win_p, seen_x, seen_pt, maps, last_maps, tiles, own, back_out, back_in,
    part_out, part_in, mean_out, count_out, count_in,
    load_sem, halo_send, halo_recv, count_send, count_recv,
    back_send, back_recv, part_send, part_recv, mean_send, mean_recv,
):
    subjects, frames = series.shape[0], series.shape[1]
    width = SPAN * BLOCK
    rows = frames // CHUNKS
    piece = rows // subj_devs
    me_s, me_c = lax.axis_index("subj"), lax.axis_index("cortex")
    left = (me_s, lax.rem(me_c + cortex_devs - 1, cortex_devs))
    right = (me_s, lax.rem(me_c + 1, cortex_devs))
    sides = (left, right)
    win_x = (win_x0, win_x1)
    peers = [lax.rem(me_s + d, subj_devs) for d in range(subj_devs)]

    barrier = pltpu.get_barrier_semaphore()
    for device in (*sides, *((p, me_c) for p in peers[1:])):
        pl.semaphore_signal(barrier, inc=1, device_id=device, device_id_type=MESH)

    loads = []
    for b in range(BLK_DEV):
        cols = pl.ds(b * BLOCK, BLOCK)
        loads.append((template.at[:, cols], win_p.at[BLK_DEV + b]))
        for s in range(subjects):
            loads.append((series.at[s, :, cols], win_x[s].at[BLK_DEV + b]))
    loads = [pltpu.make_async_copy(a, b, load_sem.at[i]) for i, (a, b) in enumerate(loads)]
    for copy in loads:
        copy.start()

    first = (me_c - 1) * BLK_DEV
    place = [
        [jnp.clip(lists[g, a] - first, 0, WIN - 1) for a in range(SPAN)] for g in range(BLK_DEV)
    ]
    entry = [
        [
            jnp.where(p[0] == w, 0, jnp.where(p[1] == w, 1, jnp.where(p[2] == w, 2, SPAN)))
            for w in range(WIN)
        ]
        for p in place
    ]
    counts = []
    for w in range(WIN):
        c = sum(jnp.where(p == w, 1.0, 0.0) for q in place for p in q)
        counts.append(jnp.full((8, BLOCK), c, jnp.float32))
    for b in range(BLK_DEV):
        count_out[0, pl.ds(8 * b, 8)] = counts[b]
        count_out[1, pl.ds(8 * b, 8)] = counts[2 * BLK_DEV + b]
    for g in range(BLK_DEV):
        tiles[g, SPAN] = jnp.zeros(tiles.shape[2:], tiles.dtype)

    pl.semaphore_wait(barrier, 2 + subj_devs - 1)

    halo = {}
    for item in range(1 + subjects):
        for side in range(2):
            for b in range(BLK_DEV):
                cols = pl.ds(b * BLOCK, BLOCK)
                spot = (2 * BLK_DEV if side == 0 else 0) + b
                if item == 0:
                    src, dst = template.at[:, cols], win_p.at[spot]
                else:
                    src, dst = series.at[item - 1, :, cols], win_x[item - 1].at[spot]
                copy = pltpu.make_async_remote_copy(
                    src, dst, halo_send.at[item, side, b], halo_recv.at[item, side, b],
                    device_id=sides[side], device_id_type=MESH,
                )
                copy.start()
                halo[item, side, b] = copy
    tally = []
    for side in range(2):
        copy = pltpu.make_async_remote_copy(
            count_out.at[side], count_in.at[side], count_send.at[side], count_recv.at[side],
            device_id=sides[side], device_id_type=MESH,
        )
        copy.start()
        tally.append(copy)
    for copy in loads:
        copy.wait()

    def arrived(item):
        for side in range(2):
            for b in range(BLK_DEV):
                halo[item, side, b].wait_recv()

    on_diagonal = lax.broadcasted_iota(jnp.int32, (width, width), 0) == lax.broadcasted_iota(
        jnp.int32, (width, width), 1
    )
    arrived(0)
    for g in range(BLK_DEV):
        for a in range(SPAN):
            seen_pt[g, pl.ds(a * BLOCK, BLOCK), :] = win_p[place[g][a]].T
    for s in range(subjects):
        arrived(1 + s)
        for g in range(BLK_DEV):
            for a in range(SPAN):
                seen_x[g, :, pl.ds((s * SPAN + a) * BLOCK, BLOCK)] = win_x[s][place[g][a]]
        for g in range(BLK_DEV):
            cross = lax.dot_general(
                seen_pt[g], seen_x[g, :, pl.ds(s * width, width)], (((1,), (0,)), ((), ())),
                preferred_element_type=jnp.float32,
            )
            cross = cross * (1.0 / frames) + jnp.where(on_diagonal, RIDGE_SHIFT, 0.0)
            scale = lax.rsqrt(jnp.sum(cross * cross, keepdims=True) + NORM_EPSILON)
            maps[g] = (cross * scale).astype(jnp.bfloat16)

        def step(_, carry):
            for g in range(BLK_DEV):
                now = maps[g]
                gram = lax.dot_general(
                    now, now, (((1,), (1,)), ((), ())), preferred_element_type=jnp.float32
                ).astype(jnp.bfloat16)
                product = lax.dot_general(
                    gram, now, (((1,), (0,)), ((), ())), preferred_element_type=jnp.float32
                )
                maps[g] = (1.5 * now.astype(jnp.float32) - 0.5 * product).astype(jnp.bfloat16)
            return carry

        lax.fori_loop(0, NS_STEPS, step, 0)
        for g in range(BLK_DEV):
            last_maps[g, :, pl.ds(s * width, width)] = maps[g]

    for copy in tally:
        copy.wait()
    shares = []
    for b in range(BLK_DEV):
        total = counts[BLK_DEV + b] + count_in[0, pl.ds(8 * b, 8)] + count_in[1, pl.ds(8 * b, 8)]
        shares.append((1.0 / (total * (subjects * subj_devs)))[0:1])
    share = jnp.concatenate(shares, axis=1)

    back = {}
    for q in range(CHUNKS):
        span = pl.ds(q * rows, rows)
        for g in range(BLK_DEV):
            mapped = lax.dot_general(
                seen_x[g, span, :], last_maps[g], (((1,), (1,)), ((), ())),
                preferred_element_type=jnp.float32,
            )
            for a in range(SPAN):
                tiles[g, a] = mapped[:, a * BLOCK : (a + 1) * BLOCK]
        for w in range(WIN):
            cols = pl.ds((w % BLK_DEV) * BLOCK, BLOCK)
            both = sum(tiles[g, entry[g][w]] for g in range(BLK_DEV))
            if w // BLK_DEV == 1:
                own[span, cols] = both
            else:
                back_out[w // (2 * BLK_DEV), span, cols] = both.astype(LINK)
        for side in range(2):
            copy = pltpu.make_async_remote_copy(
                back_out.at[side, span], back_in.at[side, span],
                back_send.at[side, q], back_recv.at[side, q],
                device_id=sides[side], device_id_type=MESH,
            )
            copy.start()
            back[side, q] = copy

    parts, means = {}, {}

    def send_parts(q):
        span = pl.ds(q * rows, rows)
        for side in range(2):
            back[side, q].wait_recv()
        total = own[span] + back_in[0, span].astype(jnp.float32) + back_in[1, span].astype(jnp.float32)
        total = total * share
        own[span] = total
        part_out[span] = total.astype(LINK)
        for d in range(1, subj_devs):
            start = pl.multiple_of(q * rows + peers[d] * piece, piece)
            copy = pltpu.make_async_remote_copy(
                part_out.at[pl.ds(start, piece)], part_in.at[d - 1, pl.ds(q * piece, piece)],
                part_send.at[d - 1, q], part_recv.at[d - 1, q],
                device_id=(peers[d], me_c), device_id_type=MESH,
            )
            copy.start()
            parts[d, q] = copy

    def send_means(q):
        span = pl.ds(q * piece, piece)
        for d in range(1, subj_devs):
            parts[d, q].wait_recv()
        start = pl.multiple_of(q * rows + me_s * piece, piece)
        total = own[pl.ds(start, piece)]
        for d in range(1, subj_devs):
            total = total + part_in[d - 1, span].astype(jnp.float32)
        mean_out[span] = total.astype(LINK)
        here = gathered.at[pl.ds(start, piece)]
        copy = pltpu.make_async_copy(mean_out.at[span], here, mean_send.at[subj_devs - 1, q])
        copy.start()
        means[0, q] = copy
        for d in range(1, subj_devs):
            copy = pltpu.make_async_remote_copy(
                mean_out.at[span], here, mean_send.at[d - 1, q], mean_recv.at[d - 1, q],
                device_id=(peers[d], me_c), device_id_type=MESH,
            )
            copy.start()
            means[d, q] = copy

    for q in range(CHUNKS):
        send_parts(q)
        if q >= 1:
            send_means(q - 1)
    send_means(CHUNKS - 1)
    for copy in halo.values():
        copy.wait_send()
    for copy in (*back.values(), *parts.values()):
        copy.wait_send()
    for copy in means.values():
        copy.wait()


def body(series, template, lists):
    subjects, frames, own_width = series.shape
    subj_devs, cortex_devs = lax.axis_size("subj"), lax.axis_size("cortex")
    width = SPAN * BLOCK
    rows = frames // CHUNKS
    piece = rows // subj_devs
    bf16, f32, dma = jnp.bfloat16, jnp.float32, pltpu.SemaphoreType.DMA
    gathered = pl.pallas_call(
        functools.partial(kernel, subj_devs, cortex_devs),
        out_shape=jax.ShapeDtypeStruct((frames, own_width), LINK),
        in_specs=[
            pl.BlockSpec(memory_space=pltpu.SMEM),
            pl.BlockSpec(memory_space=pl.ANY),
            pl.BlockSpec(memory_space=pl.ANY),
        ],
        out_specs=pl.BlockSpec(memory_space=pl.ANY),
        scratch_shapes=[
            *[pltpu.VMEM((WIN, frames, BLOCK), bf16)] * subjects,
            pltpu.VMEM((WIN, frames, BLOCK), bf16),
            pltpu.VMEM((BLK_DEV, frames, subjects * width), bf16),
            pltpu.VMEM((BLK_DEV, width, frames), bf16),
            pltpu.VMEM((BLK_DEV, width, width), bf16),
            pltpu.VMEM((BLK_DEV, width, subjects * width), bf16),
            pltpu.VMEM((BLK_DEV, SPAN + 1, rows, BLOCK), f32),
            pltpu.VMEM((frames, own_width), f32),
            pltpu.VMEM((2, frames, own_width), LINK),
            pltpu.VMEM((2, frames, own_width), LINK),
            pltpu.VMEM((frames, own_width), LINK),
            pltpu.VMEM((subj_devs - 1, CHUNKS * piece, own_width), LINK),
            pltpu.VMEM((CHUNKS * piece, own_width), LINK),
            pltpu.VMEM((2, 8 * BLK_DEV, BLOCK), f32),
            pltpu.VMEM((2, 8 * BLK_DEV, BLOCK), f32),
            dma(((1 + subjects) * BLK_DEV,)),
            dma((1 + subjects, 2, BLK_DEV)),
            dma((1 + subjects, 2, BLK_DEV)),
            dma((2,)),
            dma((2,)),
            dma((2, CHUNKS)),
            dma((2, CHUNKS)),
            dma((subj_devs - 1, CHUNKS)),
            dma((subj_devs - 1, CHUNKS)),
            dma((subj_devs, CHUNKS)),
            dma((subj_devs - 1, CHUNKS)),
        ],
        compiler_params=pltpu.CompilerParams(
            collective_id=0, has_side_effects=True, vmem_limit_bytes=48 << 20
        ),
        name="searchlights",
    )(lists, series, template)
    return gathered.astype(f32)


def solution(mesh):
    in_specs = (P("subj", None, "cortex"), P(None, "cortex"), P("cortex", None))
    out_specs = P(None, "cortex")
    return jax.shard_map(body, mesh=mesh, in_specs=in_specs, out_specs=out_specs, check_vma=False)
```

time: 226 us -> 75.9 us (0.34); the launches traced: 222 us -> 75.6 us
  waiting for transfers between devices: 95.3 us -> 0 us
  Pallas kernels: 0 us -> 71.6 us
  starting transfers between devices: 37.2 us -> 0 us
  matrix products: 32.1 us -> 0 us
  local copies, waits for them, and re-layouts: 32 us -> 2.94 us
  between operations: 13.7 us -> 0.01 us
  other arithmetic: 11.7 us -> 1.05 us
    psum x1 -> x0, waiting for transfers between devices: 86.7 us -> none  [body(): combined = lax.psum(averaged, 'subj')]
    pallas_call x0 -> x1, Pallas kernels: none -> 71.6 us  [body(): pl.pallas_call(functools.partial(kernel, subj_devs, cortex_devs), out_sha...]
    dot_general x19 -> x0, matrix products: 32.1 us -> none  [the longest x1 10.5 us: body(): jnp.einsum('sfjc,jw->sfwc', tiles, one_hot, precision=lax.Precision.HIGHEST)]
    ppermute x6 -> x0, starting transfers between devices: 20.4 us -> none  [the longest x2 9.66 us: from_behind(): return lax.ppermute(block, axis, route)]
    all_to_all x1 -> x0, starting transfers between devices: 16.7 us -> none  [copy_for_each(): lax.all_to_all(jnp.broadcast_to(x[None], (length, *x.shape)), axis, 0, 0,...]
    reshape x4 -> x0, local copies, waits for them, and re-layouts: 12.7 us -> none  [the longest x1 8.2 us: body(): tiles = mapped.reshape(subj_count, frame_count, BLK_DEV * 3, BLOCK)]
    all_to_all x1 -> x0, waiting for transfers between devices: 8.52 us -> none  [copy_for_each(): lax.all_to_all(jnp.broadcast_to(x[None], (length, *x.shape)), axis, 0, 0,...]
    gather x4 -> x0, local copies, waits for them, and re-layouts: 7.63 us -> none  [the longest x2 6.08 us: body(): jnp.take(data_blocks, window_ids, axis=2)]
  transfers between devices with their start and end apart: 8 -> 0, of which waited for: 2 -> 0; matrix products, arithmetic and copies ran while one was open for 4% -> 0% of each run, Pallas kernels for 0% -> 0%
where the time goes in v1:
time: 75.9 us; the launch traced here: 75.6 us
  Pallas kernels  71.6 us (94%)
  local copies, waits for them, and re-layouts  2.94 us (4%)
  other arithmetic  1.05 us (1%)
    pallas_call x1, Pallas kernels, body(): pl.pallas_call(functools.partial(kernel, subj_devs, cortex_devs), out_sha...  71.6 us
    unnamed x6, local copies, waits for them, and re-layouts  2.94 us

profile of v1, /device:TPU:2, one launch (start us, length us, event | category | flops | bytes accessed | tf_op | source)
XLA Modules:
  0.0 75.6 jit_solution(73030291852148843)
XLA Ops:
  0.0 0.0 copy-start
  0.0 1.2 %copy-done = bf16[2,1024,256]{2,1,0:T(8,128)(2,1)S(1)} copy-done((bf16[2,1024,256]{2,1,0:T(8,128)(2,1)S(1)}, bf16[2,1024,256]{2,1,0:T(8,128)(2,1)}, u32[]{:S(2)}) %copy-start) | copy-done | bytes 1048600
  1.2 0.0 copy-start.1
  1.2 1.0 %copy-done.1 = bf16[1024,256]{1,0:T(8,128)(2,1)S(1)} copy-done((bf16[1024,256]{1,0:T(8,128)(2,1)S(1)}, bf16[1024,256]{1,0:T(8,128)(2,1)}, u32[]{:S(2)}) %copy-start.1) | copy-done | bytes 524312
  2.3 0.0 copy-start.2
  2.3 0.7 copy-done.2
  2.9 71.6 %searchlights.1 = bf16[1024,256]{1,0:T(8,128)(2,1)S(1)} custom-call(s32[2,3]{1,0:T(2,128)S(1)} %copy-done.2, bf16[2,1024,256]{2,1,0:T(8,128)(2,1)S(1)} %copy-done, bf16[1024,256]{1,0:T(8,128)(2,1)S(1)} %copy-done.1), custom_call_target="tpu_custom_call" | custom-call | tf_op jit(solution)/shard_map/searchlights/pallas_call | solution.py:241
  74.6 1.0 %convert_element_type.3 = f32[1024,256]{1,0:T(8,128)} convert(bf16[1024,256]{1,0:T(8,128)(2,1)S(1)} %searchlights.1) | non-fusion elementwise | flops 262144 | bytes 1572864 | tf_op jit(solution)/shard_map/convert_element_type | solution.py:283
Async XLA Ops:
  0.0 1.2 %copy-start = (bf16[2,1024,256]{2,1,0:T(8,128)(2,1)S(1)}, bf16[2,1024,256]{2,1,0:T(8,128)(2,1)}, u32[]{:S(2)}) copy-start(bf16[2,1024,256]{2,1,0:T(8,128)(2,1)} %series.1) | copy-start | bytes 3145732
  1.2 1.0 %copy-start.1 = (bf16[1024,256]{1,0:T(8,128)(2,1)S(1)}, bf16[1024,256]{1,0:T(8,128)(2,1)}, u32[]{:S(2)}) copy-start(bf16[1024,256]{1,0:T(8,128)(2,1)} %template.1) | copy-start | bytes 1572868
  2.3 0.7 copy-start.2

commit v2 on v1

--- a/solution.py
+++ b/solution.py
@@ -14,20 +14,21 @@
 WIN = 3 * BLK_DEV
 RIDGE_SHIFT = 0.1
 NORM_EPSILON = 1e-06
-CHUNKS = 4
+CHUNKS = 2
+RELAYS = 4
 MESH = pl.DeviceIdType.MESH
 LINK = jnp.bfloat16
 
 
 def kernel(
-    subj_devs, cortex_devs, lists, series, template, gathered,
-    win_x0, win_x1, win_p, seen_x, seen_pt, maps, last_maps, tiles, own, back_out, back_in,
+    subj_devs, cortex_devs, lists_hbm, series, template, gathered, lists,
+    win_x0, win_x1, win_p, seen_x, seen_pt, maps, gram, last_maps, tiles, own, back_out, back_in,
     part_out, part_in, mean_out, count_out, count_in,
-    load_sem, halo_send, halo_recv, count_send, count_recv,
+    load_sem, halo_send, halo_recv, share_send, share_recv, near_send, near_recv, count_send, count_recv,
     back_send, back_recv, part_send, part_recv, mean_send, mean_recv,
 ):
     subjects, frames = series.shape[0], series.shape[1]
-    width = SPAN * BLOCK
+    width, edge = SPAN * BLOCK, (SPAN - 1) * BLOCK
     rows = frames // CHUNKS
     piece = rows // subj_devs
     me_s, me_c = lax.axis_index("subj"), lax.axis_index("cortex")
@@ -41,7 +42,7 @@
     for device in (*sides, *((p, me_c) for p in peers[1:])):
         pl.semaphore_signal(barrier, inc=1, device_id=device, device_id_type=MESH)
 
-    loads = []
+    loads = [(lists_hbm, lists)]
     for b in range(BLK_DEV):
         cols = pl.ds(b * BLOCK, BLOCK)
         loads.append((template.at[:, cols], win_p.at[BLK_DEV + b]))
@@ -50,6 +51,7 @@
     loads = [pltpu.make_async_copy(a, b, load_sem.at[i]) for i, (a, b) in enumerate(loads)]
     for copy in loads:
         copy.start()
+    loads.pop(0).wait()
 
     first = (me_c - 1) * BLK_DEV
     place = [
@@ -74,22 +76,43 @@
 
     pl.semaphore_wait(barrier, 2 + subj_devs - 1)
 
-    halo = {}
-    for item in range(1 + subjects):
+    core = lax.rem(me_c, 2)
+    near = (me_s, me_c + 1 - 2 * core)
+    far = (me_s, lax.rem(me_c - 1 + 2 * core + cortex_devs, cortex_devs))
+    turn = lax.rem(me_s, RELAYS)
+    share_rows = frames // RELAYS
+    mine = pl.ds(pl.multiple_of(turn * share_rows, share_rows), share_rows)
+    far_spot = 2 * BLK_DEV * core
+    halo, relays = {}, []
+    for b in range(BLK_DEV):
+        cols = pl.ds(b * BLOCK, BLOCK)
+        copy = pltpu.make_async_remote_copy(
+            template.at[mine, cols], win_p.at[2 * BLK_DEV - far_spot + b, mine],
+            share_send.at[0, b], share_recv.at[0, b], device_id=far, device_id_type=MESH,
+        )
+        copy.start()
+        relays.append(copy)
+    for item in range(subjects):
         for side in range(2):
             for b in range(BLK_DEV):
                 cols = pl.ds(b * BLOCK, BLOCK)
                 spot = (2 * BLK_DEV if side == 0 else 0) + b
-                if item == 0:
-                    src, dst = template.at[:, cols], win_p.at[spot]
-                else:
-                    src, dst = series.at[item - 1, :, cols], win_x[item - 1].at[spot]
                 copy = pltpu.make_async_remote_copy(
-                    src, dst, halo_send.at[item, side, b], halo_recv.at[item, side, b],
+                    series.at[item, :, cols], win_x[item].at[spot],
+                    halo_send.at[item, side, b], halo_recv.at[item, side, b],
                     device_id=sides[side], device_id_type=MESH,
                 )
                 copy.start()
                 halo[item, side, b] = copy
+        if item == 0:
+            for b in range(BLK_DEV):
+                cols = pl.ds(b * BLOCK, BLOCK)
+                copy = pltpu.make_async_remote_copy(
+                    template.at[:, cols], win_p.at[far_spot + b],
+                    near_send.at[b], near_recv.at[b], device_id=near, device_id_type=MESH,
+                )
+                copy.start()
+                halo[-1, 0, b] = copy
     tally = []
     for side in range(2):
         copy = pltpu.make_async_remote_copy(
@@ -98,6 +121,18 @@
         )
         copy.start()
         tally.append(copy)
+    for copy in list(relays):
+        copy.wait_recv()
+    for d in range(1, RELAYS):
+        peer = me_s - turn + lax.rem(turn + d, RELAYS)
+        for b in range(BLK_DEV):
+            part = win_p.at[far_spot + b, mine]
+            copy = pltpu.make_async_remote_copy(
+                part, part, share_send.at[d, b], share_recv.at[d, b],
+                device_id=(peer, me_c), device_id_type=MESH,
+            )
+            copy.start()
+            relays.append(copy)
     for copy in loads:
         copy.wait()
 
@@ -109,12 +144,15 @@
     on_diagonal = lax.broadcasted_iota(jnp.int32, (width, width), 0) == lax.broadcasted_iota(
         jnp.int32, (width, width), 1
     )
-    arrived(0)
+    for b in range(BLK_DEV):
+        halo[-1, 0, b].wait_recv()
+    for copy in relays[BLK_DEV:]:
+        copy.wait_recv()
     for g in range(BLK_DEV):
         for a in range(SPAN):
             seen_pt[g, pl.ds(a * BLOCK, BLOCK), :] = win_p[place[g][a]].T
     for s in range(subjects):
-        arrived(1 + s)
+        arrived(s)
         for g in range(BLK_DEV):
             for a in range(SPAN):
                 seen_x[g, :, pl.ds((s * SPAN + a) * BLOCK, BLOCK)] = win_x[s][place[g][a]]
@@ -129,17 +167,24 @@
 
         def step(_, carry):
             for g in range(BLK_DEV):
-                now = maps[g]
-                gram = lax.dot_general(
-                    now, now, (((1,), (1,)), ((), ())), preferred_element_type=jnp.float32
+                gram[g, :, :edge] = lax.dot_general(
+                    maps[g], maps[g, :edge], (((1,), (1,)), ((), ())),
+                    preferred_element_type=jnp.float32,
                 ).astype(jnp.bfloat16)
+            for g in range(BLK_DEV):
+                gram[g, edge:, edge:] = lax.dot_general(
+                    maps[g, edge:], maps[g, edge:], (((1,), (1,)), ((), ())),
+                    preferred_element_type=jnp.float32,
+                ).astype(jnp.bfloat16)
+                gram[g, :edge, edge:] = gram[g, edge:, :edge].T
+            for g in range(BLK_DEV):
                 product = lax.dot_general(
-                    gram, now, (((1,), (0,)), ((), ())), preferred_element_type=jnp.float32
+                    gram[g], maps[g], (((1,), (0,)), ((), ())), preferred_element_type=jnp.float32
                 )
-                maps[g] = (1.5 * now.astype(jnp.float32) - 0.5 * product).astype(jnp.bfloat16)
+                maps[g] = (1.5 * maps[g].astype(jnp.float32) - 0.5 * product).astype(jnp.bfloat16)
             return carry
 
-        lax.fori_loop(0, NS_STEPS, step, 0)
+        lax.fori_loop(0, NS_STEPS, step, 0, unroll=2)
         for g in range(BLK_DEV):
             last_maps[g, :, pl.ds(s * width, width)] = maps[g]
 
@@ -223,7 +268,7 @@
         if q >= 1:
             send_means(q - 1)
     send_means(CHUNKS - 1)
-    for copy in halo.values():
+    for copy in (*halo.values(), *relays):
         copy.wait_send()
     for copy in (*back.values(), *parts.values()):
         copy.wait_send()
@@ -242,16 +287,18 @@
         functools.partial(kernel, subj_devs, cortex_devs),
         out_shape=jax.ShapeDtypeStruct((frames, own_width), LINK),
         in_specs=[
-            pl.BlockSpec(memory_space=pltpu.SMEM),
-            pl.BlockSpec(memory_space=pl.ANY),
-            pl.BlockSpec(memory_space=pl.ANY),
+            pl.BlockSpec(memory_space=pltpu.HBM),
+            pl.BlockSpec(memory_space=pltpu.HBM),
+            pl.BlockSpec(memory_space=pltpu.HBM),
         ],
         out_specs=pl.BlockSpec(memory_space=pl.ANY),
         scratch_shapes=[
+            pltpu.SMEM((BLK_DEV, SPAN), jnp.int32),
             *[pltpu.VMEM((WIN, frames, BLOCK), bf16)] * subjects,
             pltpu.VMEM((WIN, frames, BLOCK), bf16),
             pltpu.VMEM((BLK_DEV, frames, subjects * width), bf16),
             pltpu.VMEM((BLK_DEV, width, frames), bf16),
+            pltpu.VMEM((BLK_DEV, width, width), bf16),
             pltpu.VMEM((BLK_DEV, width, width), bf16),
             pltpu.VMEM((BLK_DEV, width, subjects * width), bf16),
             pltpu.VMEM((BLK_DEV, SPAN + 1, rows, BLOCK), f32),
@@ -263,9 +310,13 @@
             pltpu.VMEM((CHUNKS * piece, own_width), LINK),
             pltpu.VMEM((2, 8 * BLK_DEV, BLOCK), f32),
             pltpu.VMEM((2, 8 * BLK_DEV, BLOCK), f32),
-            dma(((1 + subjects) * BLK_DEV,)),
-            dma((1 + subjects, 2, BLK_DEV)),
-            dma((1 + subjects, 2, BLK_DEV)),
+            dma(((1 + subjects) * BLK_DEV + 1,)),
+            dma((subjects, 2, BLK_DEV)),
+            dma((subjects, 2, BLK_DEV)),
+            dma((RELAYS, BLK_DEV)),
+            dma((RELAYS, BLK_DEV)),
+            dma((BLK_DEV,)),
+            dma((BLK_DEV,)),
             dma((2,)),
             dma((2,)),
             dma((2, CHUNKS)),
@@ -276,7 +327,7 @@
             dma((subj_devs - 1, CHUNKS)),
         ],
         compiler_params=pltpu.CompilerParams(
-            collective_id=0, has_side_effects=True, vmem_limit_bytes=48 << 20
+            collective_id=0, has_side_effects=True, vmem_limit_bytes=63 << 20
         ),
         name="searchlights",
     )(lists, series, template)

time: 75.9 us -> 65.7 us (0.87)
  Pallas kernels: 71.6 us -> 63.4 us
  local copies, waits for them, and re-layouts: 2.94 us -> 0 us
  other arithmetic: 1.05 us -> 2.09 us
    pallas_call x1, Pallas kernels: 71.6 us -> 63.4 us  [body(): pl.pallas_call(functools.partial(kernel, subj_devs, cortex_devs), out_sha...]
    unnamed x6 -> x0, local copies, waits for them, and re-layouts: 2.94 us -> none
    convert_element_type x1, other arithmetic: 1.05 us -> 2.09 us  [body(): return gathered.astype(f32)]
where the time goes in v2:
time: 65.7 us; the launch traced here: 65.5 us
  Pallas kernels  63.4 us (96%)
  other arithmetic  2.09 us (3%)
    pallas_call x1, Pallas kernels, body(): pl.pallas_call(functools.partial(kernel, subj_devs, cortex_devs), out_sha...  63.4 us
    convert_element_type x1, other arithmetic, body(): return gathered.astype(f32)  2.09 us

profile of v2, /device:TPU:2, one launch (start us, length us, event | category | flops | bytes accessed | tf_op | source)
XLA Modules:
  0.0 65.5 jit_solution(2449871308201446511)
XLA Ops:
  0.0 63.4 %searchlights.1 = bf16[1024,256]{1,0:T(8,128)(2,1)} custom-call(s32[2,3]{1,0:T(2,128)} %lists_hbm.1, bf16[2,1024,256]{2,1,0:T(8,128)(2,1)} %series.1, bf16[1024,256]{1,0:T(8,128)(2,1)} %template.1), custom_call_target="tpu_custom_call" | custom-call | tf_op jit(solution)/shard_map/searchlights/pallas_call | solution.py:286
  63.4 2.1 %convert_element_type.3 = f32[1024,256]{1,0:T(8,128)} convert(bf16[1024,256]{1,0:T(8,128)(2,1)} %searchlights.1) | non-fusion elementwise | flops 262144 | bytes 1572864 | tf_op jit(solution)/shard_map/convert_element_type | solution.py:334

commit v3 on v2

--- a/solution.py
+++ b/solution.py
@@ -14,7 +14,7 @@
 WIN = 3 * BLK_DEV
 RIDGE_SHIFT = 0.1
 NORM_EPSILON = 1e-06
-CHUNKS = 2
+CHUNKS = 4
 RELAYS = 4
 MESH = pl.DeviceIdType.MESH
 LINK = jnp.bfloat16
@@ -22,9 +22,9 @@
 
 def kernel(
     subj_devs, cortex_devs, lists_hbm, series, template, gathered, lists,
-    win_x0, win_x1, win_p, seen_x, seen_pt, maps, gram, last_maps, tiles, own, back_out, back_in,
+    win_x0, win_x1, win_p, seen_x, seen_pt, maps, gram, last_maps, spread, own, back_out, back_in,
     part_out, part_in, mean_out, count_out, count_in,
-    load_sem, halo_send, halo_recv, share_send, share_recv, near_send, near_recv, count_send, count_recv,
+    ready_sem, load_sem, halo_send, halo_recv, share_send, share_recv, near_send, near_recv, count_send, count_recv,
     back_send, back_recv, part_send, part_recv, mean_send, mean_recv,
 ):
     subjects, frames = series.shape[0], series.shape[1]
@@ -38,8 +38,12 @@
     win_x = (win_x0, win_x1)
     peers = [lax.rem(me_s + d, subj_devs) for d in range(subj_devs)]
 
+    turn = lax.rem(me_s, RELAYS)
+    mates = [me_s - turn + lax.rem(turn + d, RELAYS) for d in range(1, RELAYS)]
+    across = peers[RELAYS]
+    greeted = [*sides, *((p, me_c) for p in mates), (across, me_c)]
     barrier = pltpu.get_barrier_semaphore()
-    for device in (*sides, *((p, me_c) for p in peers[1:])):
+    for device in greeted:
         pl.semaphore_signal(barrier, inc=1, device_id=device, device_id_type=MESH)
 
     loads = [(lists_hbm, lists)]
@@ -72,14 +76,14 @@
         count_out[0, pl.ds(8 * b, 8)] = counts[b]
         count_out[1, pl.ds(8 * b, 8)] = counts[2 * BLK_DEV + b]
     for g in range(BLK_DEV):
-        tiles[g, SPAN] = jnp.zeros(tiles.shape[2:], tiles.dtype)
-
-    pl.semaphore_wait(barrier, 2 + subj_devs - 1)
+        last_maps[g, SPAN] = jnp.zeros(last_maps.shape[2:], last_maps.dtype)
+
+    pl.semaphore_wait(barrier, len(greeted))
+    pl.semaphore_signal(ready_sem, inc=1, device_id=(across, me_c), device_id_type=MESH)
 
     core = lax.rem(me_c, 2)
     near = (me_s, me_c + 1 - 2 * core)
     far = (me_s, lax.rem(me_c - 1 + 2 * core + cortex_devs, cortex_devs))
-    turn = lax.rem(me_s, RELAYS)
     share_rows = frames // RELAYS
     mine = pl.ds(pl.multiple_of(turn * share_rows, share_rows), share_rows)
     far_spot = 2 * BLK_DEV * core
@@ -92,7 +96,7 @@
         )
         copy.start()
         relays.append(copy)
-    for item in range(subjects):
+    def send_series(item):
         for side in range(2):
             for b in range(BLK_DEV):
                 cols = pl.ds(b * BLOCK, BLOCK)
@@ -104,15 +108,22 @@
                 )
                 copy.start()
                 halo[item, side, b] = copy
-        if item == 0:
+
+    def series_left(item):
+        for side in range(2):
             for b in range(BLK_DEV):
-                cols = pl.ds(b * BLOCK, BLOCK)
-                copy = pltpu.make_async_remote_copy(
-                    template.at[:, cols], win_p.at[far_spot + b],
-                    near_send.at[b], near_recv.at[b], device_id=near, device_id_type=MESH,
-                )
-                copy.start()
-                halo[-1, 0, b] = copy
+                halo[item, side, b].wait_send()
+
+    send_series(0)
+    nears = []
+    for b in range(BLK_DEV):
+        cols = pl.ds(b * BLOCK, BLOCK)
+        copy = pltpu.make_async_remote_copy(
+            template.at[:, cols], win_p.at[far_spot + b],
+            near_send.at[b], near_recv.at[b], device_id=near, device_id_type=MESH,
+        )
+        copy.start()
+        nears.append(copy)
     tally = []
     for side in range(2):
         copy = pltpu.make_async_remote_copy(
@@ -124,17 +135,19 @@
     for copy in list(relays):
         copy.wait_recv()
     for d in range(1, RELAYS):
-        peer = me_s - turn + lax.rem(turn + d, RELAYS)
         for b in range(BLK_DEV):
             part = win_p.at[far_spot + b, mine]
             copy = pltpu.make_async_remote_copy(
                 part, part, share_send.at[d, b], share_recv.at[d, b],
-                device_id=(peer, me_c), device_id_type=MESH,
+                device_id=(mates[d - 1], me_c), device_id_type=MESH,
             )
             copy.start()
             relays.append(copy)
     for copy in loads:
         copy.wait()
+    for item in range(1, subjects):
+        series_left(item - 1)
+        send_series(item)
 
     def arrived(item):
         for side in range(2):
@@ -144,9 +157,7 @@
     on_diagonal = lax.broadcasted_iota(jnp.int32, (width, width), 0) == lax.broadcasted_iota(
         jnp.int32, (width, width), 1
     )
-    for b in range(BLK_DEV):
-        halo[-1, 0, b].wait_recv()
-    for copy in relays[BLK_DEV:]:
+    for copy in (*nears, *relays[BLK_DEV:]):
         copy.wait_recv()
     for g in range(BLK_DEV):
         for a in range(SPAN):
@@ -155,10 +166,10 @@
         arrived(s)
         for g in range(BLK_DEV):
             for a in range(SPAN):
-                seen_x[g, :, pl.ds((s * SPAN + a) * BLOCK, BLOCK)] = win_x[s][place[g][a]]
+                seen_x[:, pl.ds(((g * subjects + s) * SPAN + a) * BLOCK, BLOCK)] = win_x[s][place[g][a]]
         for g in range(BLK_DEV):
             cross = lax.dot_general(
-                seen_pt[g], seen_x[g, :, pl.ds(s * width, width)], (((1,), (0,)), ((), ())),
+                seen_pt[g], seen_x[:, pl.ds((g * subjects + s) * width, width)], (((1,), (0,)), ((), ())),
                 preferred_element_type=jnp.float32,
             )
             cross = cross * (1.0 / frames) + jnp.where(on_diagonal, RIDGE_SHIFT, 0.0)
@@ -186,7 +197,8 @@
 
         lax.fori_loop(0, NS_STEPS, step, 0, unroll=2)
         for g in range(BLK_DEV):
-            last_maps[g, :, pl.ds(s * width, width)] = maps[g]
+            for a in range(SPAN):
+                last_maps[g, a, :, pl.ds(s * width, width)] = maps[g, a * BLOCK : (a + 1) * BLOCK]
 
     for copy in tally:
         copy.wait()
@@ -196,23 +208,29 @@
         shares.append((1.0 / (total * (subjects * subj_devs)))[0:1])
     share = jnp.concatenate(shares, axis=1)
 
+    for w in range(WIN):
+        for g in range(BLK_DEV):
+            spread[
+                w // BLK_DEV,
+                pl.ds((w % BLK_DEV) * BLOCK, BLOCK),
+                pl.ds(g * subjects * width, subjects * width),
+            ] = last_maps[g, entry[g][w]]
+
+    def mapped(third, span):
+        return lax.dot_general(
+            seen_x[span, :], spread[third], (((1,), (1,)), ((), ())),
+            preferred_element_type=jnp.float32,
+        )
+
     back = {}
-    for q in range(CHUNKS):
+
+    def map_sides(q):
         span = pl.ds(q * rows, rows)
-        for g in range(BLK_DEV):
-            mapped = lax.dot_general(
-                seen_x[g, span, :], last_maps[g], (((1,), (1,)), ((), ())),
-                preferred_element_type=jnp.float32,
-            )
-            for a in range(SPAN):
-                tiles[g, a] = mapped[:, a * BLOCK : (a + 1) * BLOCK]
-        for w in range(WIN):
-            cols = pl.ds((w % BLK_DEV) * BLOCK, BLOCK)
-            both = sum(tiles[g, entry[g][w]] for g in range(BLK_DEV))
-            if w // BLK_DEV == 1:
-                own[span, cols] = both
-            else:
-                back_out[w // (2 * BLK_DEV), span, cols] = both.astype(LINK)
+        for side in range(2):
+            back_out[side, span] = mapped(2 * side, span).astype(LINK)
+
+    def send_back(q):
+        span = pl.ds(q * rows, rows)
         for side in range(2):
             copy = pltpu.make_async_remote_copy(
                 back_out.at[side, span], back_in.at[side, span],
@@ -263,14 +281,23 @@
             copy.start()
             means[d, q] = copy
 
+    map_sides(0)
+    send_back(0)
+    pl.semaphore_wait(ready_sem, 1)
     for q in range(CHUNKS):
+        span = pl.ds(q * rows, rows)
+        own[span] = mapped(1, span)
+        if q < CHUNKS - 1:
+            map_sides(q + 1)
+        for side in range(2):
+            back[side, q].wait_send()
+        if q < CHUNKS - 1:
+            send_back(q + 1)
         send_parts(q)
-        if q >= 1:
-            send_means(q - 1)
-    send_means(CHUNKS - 1)
-    for copy in (*halo.values(), *relays):
-        copy.wait_send()
-    for copy in (*back.values(), *parts.values()):
+    for q in range(CHUNKS):
+        send_means(q)
+    series_left(subjects - 1)
+    for copy in (*nears, *relays, *parts.values()):
         copy.wait_send()
     for copy in means.values():
         copy.wait()
@@ -296,12 +323,12 @@
             pltpu.SMEM((BLK_DEV, SPAN), jnp.int32),
             *[pltpu.VMEM((WIN, frames, BLOCK), bf16)] * subjects,
             pltpu.VMEM((WIN, frames, BLOCK), bf16),
-            pltpu.VMEM((BLK_DEV, frames, subjects * width), bf16),
+            pltpu.VMEM((frames, BLK_DEV * subjects * width), bf16),
             pltpu.VMEM((BLK_DEV, width, frames), bf16),
             pltpu.VMEM((BLK_DEV, width, width), bf16),
             pltpu.VMEM((BLK_DEV, width, width), bf16),
-            pltpu.VMEM((BLK_DEV, width, subjects * width), bf16),
-            pltpu.VMEM((BLK_DEV, SPAN + 1, rows, BLOCK), f32),
+            pltpu.VMEM((BLK_DEV, SPAN + 1, BLOCK, subjects * width), bf16),
+            pltpu.VMEM((SPAN, BLK_DEV * BLOCK, BLK_DEV * subjects * width), bf16),
             pltpu.VMEM((frames, own_width), f32),
             pltpu.VMEM((2, frames, own_width), LINK),
             pltpu.VMEM((2, frames, own_width), LINK),
@@ -310,6 +337,7 @@
             pltpu.VMEM((CHUNKS * piece, own_width), LINK),
             pltpu.VMEM((2, 8 * BLK_DEV, BLOCK), f32),
             pltpu.VMEM((2, 8 * BLK_DEV, BLOCK), f32),
+            pltpu.SemaphoreType.REGULAR,
             dma(((1 + subjects) * BLK_DEV + 1,)),
             dma((subjects, 2, BLK_DEV)),
             dma((subjects, 2, BLK_DEV)),
@@ -327,10 +355,10 @@
             dma((subj_devs - 1, CHUNKS)),
         ],
         compiler_params=pltpu.CompilerParams(
-            collective_id=0, has_side_effects=True, vmem_limit_bytes=63 << 20
+            collective_id=0, has_side_effects=True, vmem_limit_bytes=40 << 20
         ),
         name="searchlights",
-    )(lists, series, template)
+    )(*(pltpu.with_memory_space_constraint(a, pltpu.HBM) for a in (lists, series, template)))
     return gathered.astype(f32)
 
 

time: 65.7 us -> 62.1 us (0.945)
  Pallas kernels: 63.4 us -> 60.3 us
  other arithmetic: 2.09 us -> 1.05 us
    pallas_call x1, Pallas kernels: 63.4 us -> 60.3 us  [body(): pl.pallas_call(functools.partial(kernel, subj_devs, cortex_devs), out_sha...]
    convert_element_type x1, other arithmetic: 2.09 us -> 1.05 us  [body(): return gathered.astype(f32)]
where the time goes in v3:
time: 62.1 us; the launch traced here: 61.4 us
  Pallas kernels  60.3 us (97%)
  other arithmetic  1.05 us (2%)
    pallas_call x1, Pallas kernels, body(): pl.pallas_call(functools.partial(kernel, subj_devs, cortex_devs), out_sha...  60.3 us

profile of v3, /device:TPU:2, one launch (start us, length us, event | category | flops | bytes accessed | tf_op | source)
XLA Modules:
  0.0 61.4 jit_solution(12161481033817650094)
XLA Ops:
  0.0 60.3 %searchlights.1 = bf16[1024,256]{1,0:T(8,128)(2,1)S(1)} custom-call(s32[2,3]{1,0:T(2,128)} %lists_hbm.1, bf16[2,1024,256]{2,1,0:T(8,128)(2,1)} %series.1, bf16[1024,256]{1,0:T(8,128)(2,1)} %template.1), custom_call_target="tpu_custom_call" | custom-call | tf_op jit(solution)/shard_map/searchlights/pallas_call | solution.py:313
  60.3 1.0 %convert_element_type.3 = f32[1024,256]{1,0:T(8,128)} convert(bf16[1024,256]{1,0:T(8,128)(2,1)S(1)} %searchlights.1) | non-fusion elementwise | flops 262144 | bytes 1572864 | tf_op jit(solution)/shard_map/convert_element_type | solution.py:362

commit v4 on v3

--- a/solution.py
+++ b/solution.py
@@ -14,7 +14,7 @@
 WIN = 3 * BLK_DEV
 RIDGE_SHIFT = 0.1
 NORM_EPSILON = 1e-06
-CHUNKS = 4
+CHUNKS = 2
 RELAYS = 4
 MESH = pl.DeviceIdType.MESH
 LINK = jnp.bfloat16
@@ -36,11 +36,14 @@
     right = (me_s, lax.rem(me_c + 1, cortex_devs))
     sides = (left, right)
     win_x = (win_x0, win_x1)
-    peers = [lax.rem(me_s + d, subj_devs) for d in range(subj_devs)]
-
     turn = lax.rem(me_s, RELAYS)
-    mates = [me_s - turn + lax.rem(turn + d, RELAYS) for d in range(1, RELAYS)]
-    across = peers[RELAYS]
+    half = me_s - turn
+    other = subj_devs - RELAYS - half
+    mates = [half + lax.rem(turn + d, RELAYS) for d in range(1, RELAYS)]
+    across = other + turn
+    beyond = [other + lax.rem(turn + d, RELAYS) for d in range(1, RELAYS)]
+    peers = [me_s, beyond[1], beyond[0], beyond[2], mates[1], across, mates[0], mates[2]]
+
     greeted = [*sides, *((p, me_c) for p in mates), (across, me_c)]
     barrier = pltpu.get_barrier_semaphore()
     for device in greeted:
@@ -114,6 +117,8 @@
             for b in range(BLK_DEV):
                 halo[item, side, b].wait_send()
 
+    for copy in relays:
+        copy.wait_send()
     send_series(0)
     nears = []
     for b in range(BLK_DEV):
@@ -195,7 +200,7 @@
                 maps[g] = (1.5 * maps[g].astype(jnp.float32) - 0.5 * product).astype(jnp.bfloat16)
             return carry
 
-        lax.fori_loop(0, NS_STEPS, step, 0, unroll=2)
+        lax.fori_loop(0, NS_STEPS, step, 0, unroll=4)
         for g in range(BLK_DEV):
             for a in range(SPAN):
                 last_maps[g, a, :, pl.ds(s * width, width)] = maps[g, a * BLOCK : (a + 1) * BLOCK]
@@ -297,7 +302,7 @@
     for q in range(CHUNKS):
         send_means(q)
     series_left(subjects - 1)
-    for copy in (*nears, *relays, *parts.values()):
+    for copy in (*nears, *relays[BLK_DEV:], *parts.values()):
         copy.wait_send()
     for copy in means.values():
         copy.wait()

time: 62.1 us -> 60.3 us (0.971); the launches traced: 61.4 us -> 60.3 us
  Pallas kernels: 60.3 us -> 59.2 us
    pallas_call x1, Pallas kernels: 60.3 us -> 59.2 us  [body(): pl.pallas_call(functools.partial(kernel, subj_devs, cortex_devs), out_sha...]
where the time goes in v4:
time: 60.3 us
  Pallas kernels  59.2 us (98%)
  other arithmetic  1.05 us (2%)
    pallas_call x1, Pallas kernels, body(): pl.pallas_call(functools.partial(kernel, subj_devs, cortex_devs), out_sha...  59.2 us

profile of v4, /device:TPU:2, one launch (start us, length us, event | category | flops | bytes accessed | tf_op | source)
XLA Modules:
  0.0 60.3 jit_solution(15052940475618309776)
XLA Ops:
  0.0 59.2 %searchlights.1 = bf16[1024,256]{1,0:T(8,128)(2,1)S(1)} custom-call(s32[2,3]{1,0:T(2,128)} %lists_hbm.1, bf16[2,1024,256]{2,1,0:T(8,128)(2,1)} %series.1, bf16[1024,256]{1,0:T(8,128)(2,1)} %template.1), custom_call_target="tpu_custom_call" | custom-call | tf_op jit(solution)/shard_map/searchlights/pallas_call | solution.py:318
  59.2 1.0 %convert_element_type.3 = f32[1024,256]{1,0:T(8,128)} convert(bf16[1024,256]{1,0:T(8,128)(2,1)S(1)} %searchlights.1) | non-fusion elementwise | flops 262144 | bytes 1572864 | tf_op jit(solution)/shard_map/convert_element_type | solution.py:367

commit v5 on v4

--- a/solution.py
+++ b/solution.py
@@ -14,7 +14,8 @@
 WIN = 3 * BLK_DEV
 RIDGE_SHIFT = 0.1
 NORM_EPSILON = 1e-06
-CHUNKS = 2
+SHARES = (3, 3, 2)
+CHUNKS = len(SHARES)
 RELAYS = 4
 MESH = pl.DeviceIdType.MESH
 LINK = jnp.bfloat16
@@ -29,8 +30,14 @@
 ):
     subjects, frames = series.shape[0], series.shape[1]
     width, edge = SPAN * BLOCK, (SPAN - 1) * BLOCK
-    rows = frames // CHUNKS
-    piece = rows // subj_devs
+    ends = [sum(SHARES[:q]) * frames // sum(SHARES) for q in range(CHUNKS + 1)]
+    chunks = [pl.ds(a, b - a) for a, b in zip(ends, ends[1:])]
+    slots = [pl.ds(a // subj_devs, (b - a) // subj_devs) for a, b in zip(ends, ends[1:])]
+
+    def piece(q, device):
+        rows = slots[q].size
+        return pl.ds(pl.multiple_of(ends[q] + device * rows, 16), rows)
+
     me_s, me_c = lax.axis_index("subj"), lax.axis_index("cortex")
     left = (me_s, lax.rem(me_c + cortex_devs - 1, cortex_devs))
     right = (me_s, lax.rem(me_c + 1, cortex_devs))
@@ -139,7 +146,7 @@
         tally.append(copy)
     for copy in list(relays):
         copy.wait_recv()
-    for d in range(1, RELAYS):
+    for d in (2, 1, 3):
         for b in range(BLK_DEV):
             part = win_p.at[far_spot + b, mine]
             copy = pltpu.make_async_remote_copy(
@@ -230,12 +237,12 @@
     back = {}
 
     def map_sides(q):
-        span = pl.ds(q * rows, rows)
+        span = chunks[q]
         for side in range(2):
             back_out[side, span] = mapped(2 * side, span).astype(LINK)
 
     def send_back(q):
-        span = pl.ds(q * rows, rows)
+        span = chunks[q]
         for side in range(2):
             copy = pltpu.make_async_remote_copy(
                 back_out.at[side, span], back_in.at[side, span],
@@ -248,7 +255,7 @@
     parts, means = {}, {}
 
     def send_parts(q):
-        span = pl.ds(q * rows, rows)
+        span = chunks[q]
         for side in range(2):
             back[side, q].wait_recv()
         total = own[span] + back_in[0, span].astype(jnp.float32) + back_in[1, span].astype(jnp.float32)
@@ -256,9 +263,8 @@
         own[span] = total
         part_out[span] = total.astype(LINK)
         for d in range(1, subj_devs):
-            start = pl.multiple_of(q * rows + peers[d] * piece, piece)
             copy = pltpu.make_async_remote_copy(
-                part_out.at[pl.ds(start, piece)], part_in.at[d - 1, pl.ds(q * piece, piece)],
+                part_out.at[piece(q, peers[d])], part_in.at[d - 1, slots[q]],
                 part_send.at[d - 1, q], part_recv.at[d - 1, q],
                 device_id=(peers[d], me_c), device_id_type=MESH,
             )
@@ -266,15 +272,14 @@
             parts[d, q] = copy
 
     def send_means(q):
-        span = pl.ds(q * piece, piece)
+        span = slots[q]
         for d in range(1, subj_devs):
             parts[d, q].wait_recv()
-        start = pl.multiple_of(q * rows + me_s * piece, piece)
-        total = own[pl.ds(start, piece)]
+        total = own[piece(q, me_s)]
         for d in range(1, subj_devs):
             total = total + part_in[d - 1, span].astype(jnp.float32)
         mean_out[span] = total.astype(LINK)
-        here = gathered.at[pl.ds(start, piece)]
+        here = gathered.at[piece(q, me_s)]
         copy = pltpu.make_async_copy(mean_out.at[span], here, mean_send.at[subj_devs - 1, q])
         copy.start()
         means[0, q] = copy
@@ -288,16 +293,18 @@
 
     map_sides(0)
     send_back(0)
+    map_sides(1)
+    send_back(1)
     pl.semaphore_wait(ready_sem, 1)
     for q in range(CHUNKS):
-        span = pl.ds(q * rows, rows)
+        span = chunks[q]
         own[span] = mapped(1, span)
-        if q < CHUNKS - 1:
-            map_sides(q + 1)
+        if q < CHUNKS - 2:
+            map_sides(q + 2)
         for side in range(2):
             back[side, q].wait_send()
-        if q < CHUNKS - 1:
-            send_back(q + 1)
+        if q < CHUNKS - 2:
+            send_back(q + 2)
         send_parts(q)
     for q in range(CHUNKS):
         send_means(q)
@@ -312,8 +319,6 @@
     subjects, frames, own_width = series.shape
     subj_devs, cortex_devs = lax.axis_size("subj"), lax.axis_size("cortex")
     width = SPAN * BLOCK
-    rows = frames // CHUNKS
-    piece = rows // subj_devs
     bf16, f32, dma = jnp.bfloat16, jnp.float32, pltpu.SemaphoreType.DMA
     gathered = pl.pallas_call(
         functools.partial(kernel, subj_devs, cortex_devs),
@@ -338,8 +343,8 @@
             pltpu.VMEM((2, frames, own_width), LINK),
             pltpu.VMEM((2, frames, own_width), LINK),
             pltpu.VMEM((frames, own_width), LINK),
-            pltpu.VMEM((subj_devs - 1, CHUNKS * piece, own_width), LINK),
-            pltpu.VMEM((CHUNKS * piece, own_width), LINK),
+            pltpu.VMEM((subj_devs - 1, frames // subj_devs, own_width), LINK),
+            pltpu.VMEM((frames // subj_devs, own_width), LINK),
             pltpu.VMEM((2, 8 * BLK_DEV, BLOCK), f32),
             pltpu.VMEM((2, 8 * BLK_DEV, BLOCK), f32),
             pltpu.SemaphoreType.REGULAR,

time: 60.3 us -> 59.8 us (level)
  no operation moved by 1% of the time
where the time goes in v5:
time: 59.8 us; the launch traced here: 59.7 us
  Pallas kernels  58.7 us (98%)
  other arithmetic  1.05 us (2%)
    pallas_call x1, Pallas kernels, body(): pl.pallas_call(functools.partial(kernel, subj_devs, cortex_devs), out_sha...  58.7 us

profile of v5, /device:TPU:2, one launch (start us, length us, event | category | flops | bytes accessed | tf_op | source)
XLA Modules:
  0.0 59.7 jit_solution(1669137352653582850)
XLA Ops:
  0.0 58.7 %searchlights.1 = bf16[1024,256]{1,0:T(8,128)(2,1)S(1)} custom-call(s32[2,3]{1,0:T(2,128)} %lists_hbm.1, bf16[2,1024,256]{2,1,0:T(8,128)(2,1)} %series.1, bf16[1024,256]{1,0:T(8,128)(2,1)} %template.1), custom_call_target="tpu_custom_call" | custom-call | tf_op jit(solution)/shard_map/searchlights/pallas_call | solution.py:323
  58.7 1.0 %convert_element_type.3 = f32[1024,256]{1,0:T(8,128)} convert(bf16[1024,256]{1,0:T(8,128)(2,1)S(1)} %searchlights.1) | non-fusion elementwise | flops 262144 | bytes 1572864 | tf_op jit(solution)/shard_map/convert_element_type | solution.py:372

commit v6 on v5

--- a/solution.py
+++ b/solution.py
@@ -220,13 +220,15 @@
         shares.append((1.0 / (total * (subjects * subj_devs)))[0:1])
     share = jnp.concatenate(shares, axis=1)
 
-    for w in range(WIN):
-        for g in range(BLK_DEV):
-            spread[
-                w // BLK_DEV,
-                pl.ds((w % BLK_DEV) * BLOCK, BLOCK),
-                pl.ds(g * subjects * width, subjects * width),
-            ] = last_maps[g, entry[g][w]]
+    def gather_maps(third):
+        for w in range(BLK_DEV):
+            for g in range(BLK_DEV):
+                spread[
+                    third, pl.ds(w * BLOCK, BLOCK), pl.ds(g * subjects * width, subjects * width)
+                ] = last_maps[g, entry[g][third * BLK_DEV + w]]
+
+    gather_maps(0)
+    gather_maps(2)
 
     def mapped(third, span):
         return lax.dot_general(
@@ -295,6 +297,7 @@
     send_back(0)
     map_sides(1)
     send_back(1)
+    gather_maps(1)
     pl.semaphore_wait(ready_sem, 1)
     for q in range(CHUNKS):
         span = chunks[q]

time: 59.8 us -> 59.8 us (level)
  no operation moved by 1% of the time
where the time goes in v6:
time: 59.8 us; the launch traced here: 59.7 us
  Pallas kernels  58.6 us (98%)
  other arithmetic  1.05 us (2%)
    pallas_call x1, Pallas kernels, body(): pl.pallas_call(functools.partial(kernel, subj_devs, cortex_devs), out_sha...  58.6 us

profile of v6, /device:TPU:2, one launch (start us, length us, event | category | flops | bytes accessed | tf_op | source)
XLA Modules:
  0.0 59.7 jit_solution(1432396039372645931)
XLA Ops:
  0.0 58.6 %searchlights.1 = bf16[1024,256]{1,0:T(8,128)(2,1)S(1)} custom-call(s32[2,3]{1,0:T(2,128)} %lists_hbm.1, bf16[2,1024,256]{2,1,0:T(8,128)(2,1)} %series.1, bf16[1024,256]{1,0:T(8,128)(2,1)} %template.1), custom_call_target="tpu_custom_call" | custom-call | tf_op jit(solution)/shard_map/searchlights/pallas_call | solution.py:326
  58.7 1.0 %convert_element_type.3 = f32[1024,256]{1,0:T(8,128)} convert(bf16[1024,256]{1,0:T(8,128)(2,1)S(1)} %searchlights.1) | non-fusion elementwise | flops 262144 | bytes 1572864 | tf_op jit(solution)/shard_map/convert_element_type | solution.py:375
